TPU v7x, 128 devices: a whole 4x4x4 slice. The times are simulated.
128 devices in a mesh: slab: 8 (over x, y_lo), tile: 16 (over y_hi, z, core).
Axes of the slice: x: 4, y: 4 (y_hi: 2, y_lo: 2; y = y_hi * 2 + y_lo), z: 4, core: 2. Of those that a mesh axis runs over, the one named last changes fastest.
Arguments:
- distribution_functions: float32 [19, 128, 512, 128], P(None, 'slab', 'tile')
- heat_excess_scalar: float32 [128, 512, 128], P('slab', 'tile'), may hold values from -6 to 6
- obstacle_site_flag: int32 [128, 512, 128], P('slab', 'tile'), may hold values from 0 to 1, as said below
- cabinet_category_label: int32 [1024], replicated, may hold values from 0 to 7
- intake_face_position: int32 [1024, 32], replicated, may hold values from 0 to 8388607, as said below
- outflow_face_position: int32 [1024, 32], replicated, may hold values from 0 to 8388607, as said below
- category_evolution_operator: bfloat16 [8, 2048, 2048], P(None, 'tile', 'slab'), may hold values from -0.125 to 0.125
- intake_input_coefficients: float32 [8, 2048], replicated, may hold values from -12 to 12
- outflow_output_coefficients: float32 [8, 2048], replicated, may hold values from -0.125 to 0.125
- cabinet_heat_vector: bfloat16 [1024, 2048], P('slab'), may hold values from -6 to 6
Outputs:
- new_populations: float32 [19, 128, 512, 128], P(None, 'slab', 'tile')
- new_temperature: float32 [128, 512, 128], P('slab', 'tile')
- new_states: float32 [1024, 2048], P('slab', 'tile')
Inputs may be any that keep to these rules, and one draw needn't show every extreme that they name: `intake_face_position`: each rack is a block 4 cells wide and 8 high in a row of racks along the hall; its inlet face, body and exhaust face lie in three consecutive cells along the hall's length, all within one slab of 16 cells. No cell belongs to two faces; face cells are never solid. `outflow_face_position`: same layout as the inlet faces, two cells further along the hall. `obstacle_site_flag`: the lowest and highest layer of cells and every rack body are solid.
All inputs are finite; a program needn't handle non-finite values.
Results may differ from a plain program's by a relative error of at most 0.00085.
Values may be sent and summed in bfloat16 or wider, within the bound.
A program may use at most 128 MiB of HBM per device.

v0:
```python
import jax
import jax.numpy as jnp
from jax import lax
from jax.sharding import PartitionSpec as P

STEPS = 3
VELOCITY = (
    (0, 0, 0),
    (1, 0, 0),
    (-1, 0, 0),
    (0, 1, 0),
    (0, -1, 0),
    (0, 0, 1),
    (0, 0, -1),
    (1, 1, 0),
    (-1, -1, 0),
    (1, -1, 0),
    (-1, 1, 0),
    (1, 0, 1),
    (-1, 0, -1),
    (1, 0, -1),
    (-1, 0, 1),
    (0, 1, 1),
    (0, -1, -1),
    (0, 1, -1),
    (0, -1, 1),
)
OPPOSITE = (0, 2, 1, 4, 3, 6, 5, 8, 7, 10, 9, 12, 11, 14, 13, 16, 15, 18, 17)
WEIGHTS = (1.0 / 3.0,) + (1.0 / 18.0,) * 6 + (1.0 / 36.0,) * 12
relax_time = 0.6
buoyancy = 0.01
diffusion = 0.1
mixing = 0.5
keep_share = 0.5


def extended(cells, sides, width):
    for axis, dim in sides:
        count = lax.axis_size(axis)
        head = lax.slice_in_dim(cells, 0, width, axis=dim)
        tail = lax.slice_in_dim(cells, cells.shape[dim] - width, cells.shape[dim], axis=dim)
        cells = jnp.concatenate(
            [
                lax.ppermute(tail, axis, [(i, (i + 1) % count) for i in range(count)]),
                cells,
                lax.ppermute(head, axis, [((i + 1) % count, i) for i in range(count)]),
            ],
            axis=dim,
        )
    return cells


def collide(lattice_quantities, heated_quantities, solid):
    density = jnp.sum(lattice_quantities, axis=0)
    velocity = []
    for dimension in range(3):
        summed = jnp.zeros_like(density)
        for lane in range(19):
            stride = VELOCITY[lane][dimension]
            if stride != 0:
                summed = summed + stride * lattice_quantities[lane]
        velocity.append(summed / density)
    shifted = [
        velocity[0],
        velocity[1],
        velocity[2] + relax_time * buoyancy * heated_quantities / density,
    ]
    speed_sq = shifted[0] * shifted[0] + shifted[1] * shifted[1] + shifted[2] * shifted[2]
    relaxed = []
    for lane in range(19):
        stride = VELOCITY[lane]
        projected = stride[0] * shifted[0] + stride[1] * shifted[1] + stride[2] * shifted[2]
        balance = (
            WEIGHTS[lane]
            * density
            * (1.0 + 3.0 * projected + 4.5 * projected * projected - 1.5 * speed_sq)
        )
        relaxed_lane = lattice_quantities[lane] - (lattice_quantities[lane] - balance) / relax_time
        relaxed.append(jnp.where(solid, lattice_quantities[OPPOSITE[lane]], relaxed_lane))
    return (jnp.stack(relaxed), velocity)


def heat_step(centre, neighbours, velocity, solid):
    laplace = -6.0 * centre
    carried = jnp.zeros_like(centre)
    for dimension in range(3):
        behind, ahead = neighbours[dimension]
        laplace = laplace + behind + ahead
        carried = carried + velocity[dimension] * (0.5 * (ahead - behind))
    return jnp.where(solid, centre, centre + diffusion * laplace - carried)


def advance(relaxed_pad, heat_pad, velocity, solid):
    size_x = solid.shape[0]
    size_y = solid.shape[1]
    passed = []
    for lane in range(19):
        stride = VELOCITY[lane]
        moved = relaxed_pad[
            lane, 1 - stride[0] : 1 - stride[0] + size_x, 1 - stride[1] : 1 - stride[1] + size_y
        ]
        passed.append(jnp.roll(moved, stride[2], axis=2))
    centre = heat_pad[1 : 1 + size_x, 1 : 1 + size_y]
    neighbours = (
        (heat_pad[0:size_x, 1 : 1 + size_y], heat_pad[2 : 2 + size_x, 1 : 1 + size_y]),
        (heat_pad[1 : 1 + size_x, 0:size_y], heat_pad[1 : 1 + size_x, 2 : 2 + size_y]),
        (jnp.roll(centre, 1, axis=2), jnp.roll(centre, -1, axis=2)),
    )
    return (jnp.stack(passed), heat_step(centre, neighbours, velocity, solid))


def select(products, kind_hot, rows_here):
    shaped = products.reshape(products.shape[0], kind_hot.shape[1], rows_here)
    return jnp.sum(shaped * kind_hot[:, :, None], axis=1)


def per_device(
    distribution_functions,
    heat_excess_scalar,
    obstacle_site_flag,
    cabinet_category_label,
    intake_face_position,
    outflow_face_position,
    category_evolution_operator,
    intake_input_coefficients,
    outflow_output_coefficients,
    cabinet_heat_vector,
):
    solid = obstacle_site_flag == 1
    lattice_quantities, heated_quantities = (distribution_functions, heat_excess_scalar)
    for substep in range(STEPS):
        relaxed, velocity = collide(lattice_quantities, heated_quantities, solid)
        stacked = jnp.concatenate((relaxed, heated_quantities[None]), axis=0)
        padded = extended(stacked, (("slab", 1), ("tile", 2)), 1)
        lattice_quantities, heated_quantities = advance(padded[:19], padded[19], velocity, solid)
    slab_index = lax.axis_index("slab")
    tile_index = lax.axis_index("tile")
    size_x, size_y, height = heated_quantities.shape
    across_total = size_y * lax.axis_size("tile")
    block_racks = cabinet_heat_vector.shape[0]
    kinds_count = category_evolution_operator.shape[0]
    rows_here = category_evolution_operator.shape[1]
    first_rack = slab_index * block_racks
    kind_range = jnp.arange(kinds_count, dtype=jnp.int32)
    block_types = lax.dynamic_slice_in_dim(cabinet_category_label, first_rack, block_racks)
    kind_hot = (block_types[:, None] == kind_range[None, :]).astype(jnp.float32)

    def locate(face_cells):
        pos_x = face_cells // (across_total * height)
        remain = face_cells % (across_total * height)
        pos_y = remain // height
        pos_z = remain % height
        owned = (pos_x // size_x == slab_index) & (pos_y // size_y == tile_index)
        local_index = (
            (pos_x - slab_index * size_x) * size_y + (pos_y - tile_index * size_y)
        ) * height + pos_z
        return (owned, jnp.where(owned, local_index, 0))

    flat_heat = heated_quantities.reshape(-1)
    block_inlet = lax.dynamic_slice_in_dim(intake_face_position, first_rack, block_racks, 0)
    inlet_owned, inlet_index = locate(block_inlet)
    partial_inlet = jnp.sum(jnp.where(inlet_owned, flat_heat[inlet_index], 0.0), axis=1)
    inlet_mean = lax.psum(partial_inlet, "tile") / intake_face_position.shape[1]
    piece_cols = lax.all_gather(category_evolution_operator, "slab", axis=2, tiled=True)
    flat_piece = piece_cols.reshape(kinds_count * rows_here, piece_cols.shape[2])
    all_kinds = lax.dot_general(
        cabinet_heat_vector,
        flat_piece,
        (((1,), (1,)), ((), ())),
        preferred_element_type=jnp.float32,
    )
    mixed = select(all_kinds, kind_hot, rows_here)
    first_row = tile_index * rows_here
    state_rows = lax.dynamic_slice_in_dim(cabinet_heat_vector, first_row, rows_here, 1).astype(
        jnp.float32
    )
    gain_table = lax.dynamic_slice_in_dim(intake_input_coefficients, first_row, rows_here, 1)
    read_table = lax.dynamic_slice_in_dim(outflow_output_coefficients, first_row, rows_here, 1)
    gain_rows = jnp.dot(kind_hot, gain_table, precision=lax.Precision.HIGHEST)
    read_rows = jnp.dot(kind_hot, read_table, precision=lax.Precision.HIGHEST)
    new_states = keep_share * state_rows + mixed + gain_rows * inlet_mean[:, None]
    partial_exhaust = jnp.sum(read_rows * new_states, axis=1)
    exhaust = lax.psum(partial_exhaust, "tile")
    block_exhaust = lax.dynamic_slice_in_dim(outflow_face_position, first_rack, block_racks, 0)
    exhaust_owned, exhaust_index = locate(block_exhaust)
    old_values = flat_heat[exhaust_index]
    change = jnp.where(exhaust_owned, mixing * (exhaust[:, None] - old_values), 0.0)
    flat_heat = flat_heat.at[exhaust_index.reshape(-1)].add(change.reshape(-1))
    return (lattice_quantities, flat_heat.reshape(heated_quantities.shape), new_states)


def solution(mesh):
    return jax.shard_map(
        per_device,
        mesh=mesh,
        in_specs=(
            P(None, "slab", "tile", None),
            P("slab", "tile", None),
            P("slab", "tile", None),
            P(),
            P(),
            P(),
            P(None, "tile", "slab"),
            P(),
            P(),
            P("slab", None),
        ),
        out_specs=(P(None, "slab", "tile", None), P("slab", "tile", None), P("slab", "tile")),
        check_vma=False,
    )
```

profile of v0, /device:TPU:7, one launch (start us, length us, event | category | flops | bytes accessed | tf_op | source)
XLA Modules:
  0.0 359.1 jit_solution(3612530613693756231)
XLA Ops:
  7.2 3.0 reduce_sum.184
  10.3 4.1 %bitcast_dynamic-update-slice_fusion.10 = (f32[20,16,32,128]{3,2,1,0:T(8,128)S(1)}, f32[16,32,128]{2,1,0:T(8,128)}, f32[16,32,128]{2,1,0:T(8,128)S(1)}, f32[16,3...) fusion(f32[16,32,128]{2,1,0:T(8,128)S(1)} %reduce_sum.184, ...), kind=kLoop, calls=%fused_computation.703 | loop fusion | flops 4521983 | bytes 7667712
  19.7 2.3 copy-done.4
  26.9 15.5 %collective-permute-done = f32[20,1,32,128]{3,2,1,0:T(8,128)S(1)} collective-permute-done((f32[20,1,32,128]{3,2,1,0:T(8,128)S(1)}, f32[20,1,32,128]{3,2,1,0:T(8,128)S(1)}, u32[]{:S(2)}, u32[]{:S(2)}) %collective-permute-start) | collective-permute-done | bytes 327712 | tf_op jit(solution)/shard_map/ppermute | solution.py:44
  42.5 4.2 %collective-permute-done.1 = f32[20,1,32,128]{3,2,1,0:T(8,128)S(1)} collective-permute-done((f32[20,1,32,128]{3,2,1,0:T(8,128)S(1)}, f32[20,1,32,128]{3,2,1,0:T(8,128)S(1)}, u32[]{:S(2)}, u32[]{:S(2)}) %collective-permute-start.1) | collective-permute-done | bytes 327712 | tf_op jit(solution)/shard_map/ppermute | solution.py:46
  46.7 2.9 pad_maximum_fusion.70
  49.5 2.5 collective-permute-start.2
  60.5 4.0 %bitcast_dynamic-update-slice_fusion.6 = (f32[20,16,32,128]{3,2,1,0:T(8,128)S(1)}, f32[16,32,128]{2,1,0:T(8,128)}, f32[16,32,128]{2,1,0:T(8,128)S(1)}, f32[16,32...) fusion(pred[16,32,128]{2,1,0:T(8,128)(4,1)S(1)} %get-tuple-elem, ...), kind=kLoop, calls=%fused_computation.699 | loop fusion | flops 9175039 | bytes 18653184
  68.7 2.3 copy-done.3
  75.1 12.0 %collective-permute-done.4 = f32[20,1,32,128]{3,2,1,0:T(8,128)S(1)} collective-permute-done((f32[20,1,32,128]{3,2,1,0:T(8,128)S(1)}, f32[20,1,32,128]{3,2,1,0:T(8,128)S(1)}, u32[]{:S(2)}, u32[]{:S(2)}) %collective-permute-start.4) | collective-permute-done | bytes 327712 | tf_op jit(solution)/shard_map/ppermute | solution.py:44
  87.1 9.8 %collective-permute-done.5 = f32[20,1,32,128]{3,2,1,0:T(8,128)S(1)} collective-permute-done((f32[20,1,32,128]{3,2,1,0:T(8,128)S(1)}, f32[20,1,32,128]{3,2,1,0:T(8,128)S(1)}, u32[]{:S(2)}, u32[]{:S(2)}) %collective-permute-start.5) | collective-permute-done | bytes 327712 | tf_op jit(solution)/shard_map/ppermute | solution.py:46
  96.9 2.8 pad_maximum_fusion.67
  99.7 12.5 %collective-permute-start.6 = (f32[20,18,1,128]{3,2,1,0:T(1,128)}, f32[20,18,1,128]{3,2,1,0:T(1,128)S(1)}, u32[]{:S(2)}, u32[]{:S(2)}) collective-permute-start(f32[20,18,1,128]{3,2,1,0:T(1,128)} %get-tuple-element.107), channel_id=1, source_target_pairs={{0,1},{1,2},{2,3},{3,4},{4,5},{5,6},{6,7},{7,8},{8,9},{9,10},{10,1... | collective-permute-start | bytes 552968 | tf_op jit(solution)/shard_map/ppermute | solution.py:44
  120.7 3.4 constant_dynamic-update-slice_fusion
  128.3 6.5 %collective-permute-start.9 = (f32[20,1,32,128]{3,2,1,0:T(8,128)S(1)}, f32[20,1,32,128]{3,2,1,0:T(8,128)S(1)}, u32[]{:S(2)}, u32[]{:S(2)}) collective-permute-start(f32[20,1,32,128]{3,2,1,0:T(8,128)S(1)} %get-tuple-element.123), channel_id=1, source_target_pairs={{16,0},{32,16},{48,32},{64,48},{80,64},{96,80},{112,96},{0,112},{1... | collective-permute-start | bytes 983048 | tf_op jit(solution)/shard_map/ppermute | solution.py:46
  136.5 9.8 %collective-permute-done.8 = f32[20,1,32,128]{3,2,1,0:T(8,128)S(1)} collective-permute-done((f32[20,1,32,128]{3,2,1,0:T(8,128)S(1)}, f32[20,1,32,128]{3,2,1,0:T(8,128)S(1)}, u32[]{:S(2)}, u32[]{:S(2)}) %collective-permute-start.8) | collective-permute-done | bytes 327712 | tf_op jit(solution)/shard_map/ppermute | solution.py:44
  146.2 2.6 collective-permute-done.9
  151.4 13.0 %collective-permute-start.11 = (f32[20,18,1,128]{3,2,1,0:T(1,128)S(1)}, f32[20,18,1,128]{3,2,1,0:T(1,128)S(1)}, u32[]{:S(2)}, u32[]{:S(2)}) collective-permute-start(f32[20,18,1,128]{3,2,1,0:T(1,128)S(1)} %get-tuple-element.103), channel_id=1, source_target_pairs={{1,0},{2,1},{3,2},{4,3},{5,4},{6,5},{7,6},{8,7},{9,8},{10,9},{11,1... | collective-permute-start | bytes 552968 | tf_op jit(solution)/shard_map/ppermute | solution.py:46
  166.6 23.0 %gather_fusion = f32[4096]{0:T(1024)S(1)} fusion(f32[65536]{0:T(1024)S(1)} %bitcast.598, s32[4096]{0:T(1024)S(1)} %copy-done.24), kind=kCustom, calls=%fused_computation | custom fusion | bytes 49152 | tf_op jit(solution)/shard_map/gather | solution.py:162
  189.7 23.0 %gather_fusion.1 = f32[4096]{0:T(1024)S(1)} fusion(f32[65536]{0:T(1024)S(1)} %bitcast.599, s32[4096]{0:T(1024)S(1)} %get-tuple-element.143), kind=kCustom, calls=%fused_computation.1 | custom fusion | bytes 49152 | tf_op jit(solution)/shard_map/gather | solution.py:186
  226.1 39.8 %psum.14 = f32[128]{0:T(128)S(1)} all-reduce(f32[128]{0:T(128)S(1)} %select_reduce_fusion), channel_id=1, replica_groups=mesh['slab'=8,'tile'=16] {'tile'}, use_global_device_ids=true, to_apply=%region_3.4 | all-reduce | flops 128 | bytes 1024 | tf_op jit(solution)/shard_map/psum | solution.py:163
  277.6 3.7 %fusion = f32[128,128]{1,0:T(8,128)S(1)} fusion(bf16[8,128,2048]{2,1,0:T(8,128)(2,1)} %all-gather.2.cloned.1.call-done, bf16[128,2048]{1,0:T(8,128)(2,1)S(1)} %copy-done, f32[128,8]{0,1:T(8,128)S(1)} %fusion.571), kind=kOutput, calls=%fused_computation.4 | convolution fusion | flops 537116672 | bytes 4788224 | tf_op jit(solution)/shard_map/dot_general | solution.py:166
  284.0 38.5 %psum.15 = f32[128]{0:T(128)S(1)} all-reduce(f32[128]{0:T(128)S(1)} %fusion.2), channel_id=1, replica_groups=mesh['slab'=8,'tile'=16] {'tile'}, use_global_device_ids=true, to_apply=%region_5.6 | all-reduce | flops 128 | bytes 1024 | tf_op jit(solution)/shard_map/psum | solution.py:183
  322.7 28.9 %scatter_fusion = f32[65536]{0:T(1024)S(1)} fusion(f32[65536]{0:T(1024)S(1)} %bitcast.600, s32[4096]{0:T(1024)S(1)} %bitcast.638, f32[4096]{0:T(1024)S(1)} %reshape.165), kind=kCustom, calls=%fused_computation.2 | custom fusion | flops 4096 | bytes 65536 | tf_op jit(solution)/shard_map/scatter-add | solution.py:188
  (243 shorter events, 73.9 us)
Async XLA Ops:
  7.2 105.0 %copy-start = (bf16[128,2048]{1,0:T(8,128)(2,1)S(1)}, bf16[128,2048]{1,0:T(8,128)(2,1)}, u32[]{:S(2)}) copy-start(bf16[128,2048]{1,0:T(8,128)(2,1)} %param.19) | copy-start | bytes 1572868
  7.2 270.4 %all-gather.2.cloned.1.call-start = ((), (), s32[]{:S(2)}) async-start(), calls=%async_computation | async-start | bytes 4718592 | tf_op jit(solution)/shard_map/all_gather | solution.py:164
  16.6 37.0 %copy-start.6 = (f32[16,32,128]{2,1,0:T(8,128)}, f32[16,32,128]{2,1,0:T(8,128)S(1)}, u32[]{:S(2)}) copy-start(f32[16,32,128]{2,1,0:T(8,128)S(1)} %get-tuple-element.80) | copy-start | bytes 786436
  16.8 35.9 %copy-start.10 = (f32[16,32,128]{2,1,0:T(8,128)}, f32[16,32,128]{2,1,0:T(8,128)S(1)}, u32[]{:S(2)}) copy-start(f32[16,32,128]{2,1,0:T(8,128)S(1)} %get-tuple-element.78) | copy-start | bytes 786436
  22.1 20.4 %collective-permute-start = (f32[20,1,32,128]{3,2,1,0:T(8,128)S(1)}, f32[20,1,32,128]{3,2,1,0:T(8,128)S(1)}, u32[]{:S(2)}, u32[]{:S(2)}) collective-permute-start(f32[20,1,32,128]{3,2,1,0:T(8,128)S(1)} %get-tuple-element.129), channel_id=1, source_target_pairs={{0,16},{16,32},{32,48},{48,64},{64,80},{80,96},{96,112},{112,0},{1... | collective-permute-start | bytes 983048 | tf_op jit(solution)/shard_map/ppermute | solution.py:44
  23.5 23.2 %collective-permute-start.1 = (f32[20,1,32,128]{3,2,1,0:T(8,128)S(1)}, f32[20,1,32,128]{3,2,1,0:T(8,128)S(1)}, u32[]{:S(2)}, u32[]{:S(2)}) collective-permute-start(f32[20,1,32,128]{3,2,1,0:T(8,128)S(1)} %get-tuple-element.130), channel_id=1, source_target_pairs={{16,0},{32,16},{48,32},{64,48},{80,64},{96,80},{112,96},{0,112},{1... | collective-permute-start | bytes 983048 | tf_op jit(solution)/shard_map/ppermute | solution.py:46
  46.7 10.9 %slice-start.4 = ((s8[5242880]{0:T(1024)(128)(4,1)}), s8[1048576]{0:T(1024)(128)(4,1)S(1)}, s32[]{:S(2)}) async-start(s8[5242880]{0:T(1024)(128)(4,1)} %bitcast.606), calls=%async_computation.5 | async-start | bytes 2097152
  49.5 7.4 %collective-permute-start.2 = (f32[20,18,1,128]{3,2,1,0:T(1,128)}, f32[20,18,1,128]{3,2,1,0:T(1,128)S(1)}, u32[]{:S(2)}, u32[]{:S(2)}) collective-permute-start(f32[20,18,1,128]{3,2,1,0:T(1,128)} %get-tuple-element.111), channel_id=1, source_target_pairs={{0,1},{1,2},{2,3},{3,4},{4,5},{5,6},{6,7},{7,8},{8,9},{9,10},{10,1... | collective-permute-start | bytes 552968 | tf_op jit(solution)/shard_map/ppermute | solution.py:44
  52.0 5.6 %collective-permute-start.3 = (f32[20,18,1,128]{3,2,1,0:T(1,128)}, f32[20,18,1,128]{3,2,1,0:T(1,128)}, u32[]{:S(2)}, u32[]{:S(2)}) collective-permute-start(f32[20,18,1,128]{3,2,1,0:T(1,128)} %get-tuple-element.112), channel_id=1, source_target_pairs={{1,0},{2,1},{3,2},{4,3},{5,4},{6,5},{7,6},{8,7},{9,8},{10,9},{11,1... | collective-permute-start | bytes 552968 | tf_op jit(solution)/shard_map/ppermute | solution.py:46
  65.7 49.5 %copy-start.8 = (f32[16,32,128]{2,1,0:T(8,128)}, f32[16,32,128]{2,1,0:T(8,128)S(1)}, u32[]{:S(2)}) copy-start(f32[16,32,128]{2,1,0:T(8,128)S(1)} %get-tuple-element.50) | copy-start | bytes 786436
  65.9 49.1 %copy-start.12 = (f32[16,32,128]{2,1,0:T(8,128)}, f32[16,32,128]{2,1,0:T(8,128)S(1)}, u32[]{:S(2)}) copy-start(f32[16,32,128]{2,1,0:T(8,128)S(1)} %get-tuple-element.48) | copy-start | bytes 786436
  71.0 16.1 %collective-permute-start.4 = (f32[20,1,32,128]{3,2,1,0:T(8,128)S(1)}, f32[20,1,32,128]{3,2,1,0:T(8,128)S(1)}, u32[]{:S(2)}, u32[]{:S(2)}) collective-permute-start(f32[20,1,32,128]{3,2,1,0:T(8,128)S(1)} %get-tuple-element.126), channel_id=1, source_target_pairs={{0,16},{16,32},{32,48},{48,64},{64,80},{80,96},{96,112},{112,0},{1... | collective-permute-start | bytes 983048 | tf_op jit(solution)/shard_map/ppermute | solution.py:44
  72.7 24.2 %collective-permute-start.5 = (f32[20,1,32,128]{3,2,1,0:T(8,128)S(1)}, f32[20,1,32,128]{3,2,1,0:T(8,128)S(1)}, u32[]{:S(2)}, u32[]{:S(2)}) collective-permute-start(f32[20,1,32,128]{3,2,1,0:T(8,128)S(1)} %get-tuple-element.127), channel_id=1, source_target_pairs={{16,0},{32,16},{48,32},{64,48},{80,64},{96,80},{112,96},{0,112},{1... | collective-permute-start | bytes 983048 | tf_op jit(solution)/shard_map/ppermute | solution.py:46
  99.7 17.8 %slice-start.2 = ((s8[5242880]{0:T(1024)(128)(4,1)}), s8[1048576]{0:T(1024)(128)(4,1)S(1)}, s32[]{:S(2)}) async-start(s8[5242880]{0:T(1024)(128)(4,1)} %bitcast.604), calls=%async_computation.3 | async-start | bytes 2097152
  99.7 17.5 %collective-permute-start.6 = (f32[20,18,1,128]{3,2,1,0:T(1,128)}, f32[20,18,1,128]{3,2,1,0:T(1,128)S(1)}, u32[]{:S(2)}, u32[]{:S(2)}) collective-permute-start(f32[20,18,1,128]{3,2,1,0:T(1,128)} %get-tuple-element.107), channel_id=1, source_target_pairs={{0,1},{1,2},{2,3},{3,4},{4,5},{5,6},{6,7},{7,8},{8,9},{9,10},{10,1... | collective-permute-start | bytes 552968 | tf_op jit(solution)/shard_map/ppermute | solution.py:44
  112.2 5.3 %collective-permute-start.7 = (f32[20,18,1,128]{3,2,1,0:T(1,128)}, f32[20,18,1,128]{3,2,1,0:T(1,128)}, u32[]{:S(2)}, u32[]{:S(2)}) collective-permute-start(f32[20,18,1,128]{3,2,1,0:T(1,128)} %get-tuple-element.108), channel_id=1, source_target_pairs={{1,0},{2,1},{3,2},{4,3},{5,4},{6,5},{7,6},{8,7},{9,8},{10,9},{11,1... | collective-permute-start | bytes 552968 | tf_op jit(solution)/shard_map/ppermute | solution.py:46
  128.1 37.8 %copy-start.2 = (f32[20,16,32,128]{3,2,1,0:T(8,128)}, f32[20,16,32,128]{3,2,1,0:T(8,128)S(1)}, u32[]{:S(2)}) copy-start(f32[20,16,32,128]{3,2,1,0:T(8,128)S(1)} %bitcast_dynamic-update-slice_fusion) | copy-start | bytes 15728644
  128.2 18.1 %collective-permute-start.8 = (f32[20,1,32,128]{3,2,1,0:T(8,128)S(1)}, f32[20,1,32,128]{3,2,1,0:T(8,128)S(1)}, u32[]{:S(2)}, u32[]{:S(2)}) collective-permute-start(f32[20,1,32,128]{3,2,1,0:T(8,128)S(1)} %get-tuple-element.124), channel_id=1, source_target_pairs={{0,16},{16,32},{32,48},{48,64},{64,80},{80,96},{96,112},{112,0},{1... | collective-permute-start | bytes 983048 | tf_op jit(solution)/shard_map/ppermute | solution.py:44
  128.3 20.6 %collective-permute-start.9 = (f32[20,1,32,128]{3,2,1,0:T(8,128)S(1)}, f32[20,1,32,128]{3,2,1,0:T(8,128)S(1)}, u32[]{:S(2)}, u32[]{:S(2)}) collective-permute-start(f32[20,1,32,128]{3,2,1,0:T(8,128)S(1)} %get-tuple-element.123), channel_id=1, source_target_pairs={{16,0},{32,16},{48,32},{64,48},{80,64},{96,80},{112,96},{0,112},{1... | collective-permute-start | bytes 983048 | tf_op jit(solution)/shard_map/ppermute | solution.py:46
  149.1 16.8 %collective-permute-start.10 = (f32[20,18,1,128]{3,2,1,0:T(1,128)S(1)}, f32[20,18,1,128]{3,2,1,0:T(1,128)S(1)}, u32[]{:S(2)}, u32[]{:S(2)}) collective-permute-start(f32[20,18,1,128]{3,2,1,0:T(1,128)S(1)} %get-tuple-element.104), channel_id=1, source_target_pairs={{0,1},{1,2},{2,3},{3,4},{4,5},{5,6},{6,7},{7,8},{8,9},{9,10},{10,1... | collective-permute-start | bytes 552968 | tf_op jit(solution)/shard_map/ppermute | solution.py:44
  151.4 14.5 %collective-permute-start.11 = (f32[20,18,1,128]{3,2,1,0:T(1,128)S(1)}, f32[20,18,1,128]{3,2,1,0:T(1,128)S(1)}, u32[]{:S(2)}, u32[]{:S(2)}) collective-permute-start(f32[20,18,1,128]{3,2,1,0:T(1,128)S(1)} %get-tuple-element.103), channel_id=1, source_target_pairs={{1,0},{2,1},{3,2},{4,3},{5,4},{6,5},{7,6},{8,7},{9,8},{10,9},{11,1... | collective-permute-start | bytes 552968 | tf_op jit(solution)/shard_map/ppermute | solution.py:46
  267.8 13.6 %copy-start.28 = (bf16[128,128]{0,1:T(8,128)(2,1)S(1)}, bf16[128,128]{0,1:T(8,128)(2,1)}, u32[]{:S(2)}) copy-start(bf16[128,128]{0,1:T(8,128)(2,1)} %copy.25) | copy-start | bytes 98308
  267.8 54.8 %copy-start.31 = (pred[128,32]{1,0:T(8,128)(4,1)S(1)}, pred[128,32]{1,0:T(8,128)(4,1)}, u32[]{:S(2)}) copy-start(pred[128,32]{1,0:T(8,128)(4,1)} %get-tuple-element.16) | copy-start | bytes 12292
  269.7 53.0 %copy-start.29 = (s32[4096,1]{0,1:T(1,128)S(1)}, s32[4096,1]{0,1:T(1,128)}, u32[]{:S(2)}) copy-start(s32[4096,1]{0,1:T(1,128)} %compare_select_fusion.2) | copy-start | bytes 49156
  (27 other events, 78.7 us)
Sparse Core Ops, SparseCore 0:
  24.7 122.2 all-gather.1
where the time goes:
time: 360 us; the launch traced here: 359 us
  other arithmetic  93.7 us (26%)
  blocking collectives  78.3 us (22%)
  local copies, waits for them, and re-layouts  69.8 us (19%)
  waiting for transfers between devices  54.9 us (15%)
  starting transfers between devices  41.8 us (12%)
  between operations  15 us (4%)
  matrix products  5.62 us (2%)
    unnamed x75, other arithmetic  43.6 us
    psum x1, blocking collectives, per_device(): inlet_mean = lax.psum(partial_inlet, 'tile') / intake_face_position.shape[1]  39.8 us
    psum x1, blocking collectives, per_device(): exhaust = lax.psum(partial_exhaust, 'tile')  38.5 us
    ppermute x6, waiting for transfers between devices, extended(): lax.ppermute(tail, axis, [(i, (i + 1) % count) for i in range(count)])  37.3 us
    scatter-add x1, other arithmetic, per_device(): flat_heat = flat_heat.at[exhaust_index.reshape(-1)].add(change.reshape(-1))  28.9 us
    gather x2, local copies, waits for them, and re-layouts, per_device(): flat_heat[inlet_index]  23.1 us
    gather x2, local copies, waits for them, and re-layouts, per_device(): old_values = flat_heat[exhaust_index]  23.1 us
    ppermute x6, starting transfers between devices, extended(): lax.ppermute(head, axis, [((i + 1) % count, i) for i in range(count)])  21.4 us
  transfers between devices with their start and end apart: 13, of which 8 were waited for; matrix products, arithmetic and copies ran while one was open for 32% of the time, Pallas kernels for 0%

commit v1 on v0

--- a/solution.py
+++ b/solution.py
@@ -180,7 +180,8 @@
     read_rows = jnp.dot(kind_hot, read_table, precision=lax.Precision.HIGHEST)
     new_states = keep_share * state_rows + mixed + gain_rows * inlet_mean[:, None]
     partial_exhaust = jnp.sum(read_rows * new_states, axis=1)
-    exhaust = lax.psum(partial_exhaust, "tile")
+    pieces = lax.all_gather(partial_exhaust, "tile", axis=0, tiled=False)
+    exhaust = pieces.sum(axis=0)
     block_exhaust = lax.dynamic_slice_in_dim(outflow_face_position, first_rack, block_racks, 0)
     exhaust_owned, exhaust_index = locate(block_exhaust)
     old_values = flat_heat[exhaust_index]

time: 360 us -> 347 us (0.964)
  blocking collectives: 78.3 us -> 64.5 us
  starting transfers between devices: 41.8 us -> 37.2 us
    psum x1 -> x0, blocking collectives: 38.5 us -> none  [per_device(): exhaust = lax.psum(partial_exhaust, 'tile')]
    all_gather x0 -> x1, blocking collectives: none -> 24.6 us  [per_device(): pieces = lax.all_gather(partial_exhaust, 'tile', axis=0, tiled=False)]
    ppermute x6, waiting for transfers between devices: 37.3 us -> 48.9 us  [extended(): lax.ppermute(tail, axis, [(i, (i + 1) % count) for i in range(count)])]
    ppermute x6, waiting for transfers between devices: 17.6 us -> 6.98 us  [extended(): lax.ppermute(head, axis, [((i + 1) % count, i) for i in range(count)])]
    unnamed x81 -> x83, local copies, waits for them, and re-layouts: 9.84 us -> 10.1 us
  transfers between devices with their start and end apart: 13 -> 13, of which waited for: 8 -> 6; matrix products, arithmetic and copies ran while one was open for 32% -> 34% of each run, Pallas kernels for 0% -> 0%
where the time goes in v1:
time: 347 us; the launch traced here: 343 us
  other arithmetic  93.6 us (27%)
  local copies, waits for them, and re-layouts  70.8 us (20%)
  blocking collectives  64.5 us (19%)
  waiting for transfers between devices  55.9 us (16%)
  starting transfers between devices  37.2 us (11%)
  between operations  15 us (4%)
  matrix products  5.61 us (2%)
    ppermute x6, waiting for transfers between devices, extended(): lax.ppermute(tail, axis, [(i, (i + 1) % count) for i in range(count)])  48.9 us
    unnamed x75, other arithmetic  43.6 us
    psum x1, blocking collectives, per_device(): inlet_mean = lax.psum(partial_inlet, 'tile') / intake_face_position.shape[1]  39.9 us
    scatter-add x1, other arithmetic, per_device(): flat_heat = flat_heat.at[exhaust_index.reshape(-1)].add(change.reshape(-1))  28.9 us
    all_gather x1, blocking collectives, per_device(): pieces = lax.all_gather(partial_exhaust, 'tile', axis=0, tiled=False)  24.6 us
    gather x2, local copies, waits for them, and re-layouts, per_device(): flat_heat[inlet_index]  23.1 us
    gather x2, local copies, waits for them, and re-layouts, per_device(): old_values = flat_heat[exhaust_index]  23.1 us
    ppermute x6, starting transfers between devices, extended(): lax.ppermute(tail, axis, [(i, (i + 1) % count) for i in range(count)])  18.9 us
  transfers between devices with their start and end apart: 13, of which 6 were waited for; matrix products, arithmetic and copies ran while one was open for 34% of the time, Pallas kernels for 0%

profile of v1, /device:TPU:7, one launch (start us, length us, event | category | flops | bytes accessed | tf_op | source)
XLA Modules:
  0.0 342.7 jit_solution(14094817974932600)
XLA Ops:
  7.2 3.0 reduce_sum.193
  10.3 4.1 %bitcast_dynamic-update-slice_fusion.10 = (f32[20,16,32,128]{3,2,1,0:T(8,128)S(1)}, f32[16,32,128]{2,1,0:T(8,128)}, f32[16,32,128]{2,1,0:T(8,128)S(1)}, f32[16,3...) fusion(f32[16,32,128]{2,1,0:T(8,128)S(1)} %reduce_sum.193, ...), kind=kLoop, calls=%fused_computation.703 | loop fusion | flops 4521983 | bytes 7667712
  19.7 2.3 copy-done.4
  27.7 14.8 %collective-permute-done = f32[20,1,32,128]{3,2,1,0:T(8,128)S(1)} collective-permute-done((f32[20,1,32,128]{3,2,1,0:T(8,128)S(1)}, f32[20,1,32,128]{3,2,1,0:T(8,128)S(1)}, u32[]{:S(2)}, u32[]{:S(2)}) %collective-permute-start) | collective-permute-done | bytes 327712 | tf_op jit(solution)/shard_map/ppermute | solution.py:44
  42.5 4.2 %collective-permute-done.1 = f32[20,1,32,128]{3,2,1,0:T(8,128)S(1)} collective-permute-done((f32[20,1,32,128]{3,2,1,0:T(8,128)S(1)}, f32[20,1,32,128]{3,2,1,0:T(8,128)S(1)}, u32[]{:S(2)}, u32[]{:S(2)}) %collective-permute-start.1) | collective-permute-done | bytes 327712 | tf_op jit(solution)/shard_map/ppermute | solution.py:46
  46.7 2.8 pad_maximum_fusion.70
  49.5 2.5 collective-permute-start.2
  61.4 4.0 %bitcast_dynamic-update-slice_fusion.6 = (f32[20,16,32,128]{3,2,1,0:T(8,128)S(1)}, f32[16,32,128]{2,1,0:T(8,128)}, f32[16,32,128]{2,1,0:T(8,128)S(1)}, f32[16,32...) fusion(pred[16,32,128]{2,1,0:T(8,128)(4,1)S(1)} %get-tuple-elem, ...), kind=kLoop, calls=%fused_computation.699 | loop fusion | flops 9175039 | bytes 18653184
  69.5 2.3 copy-done.3
  75.0 24.5 %collective-permute-done.4 = f32[20,1,32,128]{3,2,1,0:T(8,128)S(1)} collective-permute-done((f32[20,1,32,128]{3,2,1,0:T(8,128)S(1)}, f32[20,1,32,128]{3,2,1,0:T(8,128)S(1)}, u32[]{:S(2)}, u32[]{:S(2)}) %collective-permute-start.4) | collective-permute-done | bytes 327712 | tf_op jit(solution)/shard_map/ppermute | solution.py:44
  99.5 2.7 pad_maximum_fusion.67
  102.2 10.4 %collective-permute-start.6 = (f32[20,18,1,128]{3,2,1,0:T(1,128)}, f32[20,18,1,128]{3,2,1,0:T(1,128)S(1)}, u32[]{:S(2)}, u32[]{:S(2)}) collective-permute-start(f32[20,18,1,128]{3,2,1,0:T(1,128)} %get-tuple-element.107), channel_id=1, source_target_pairs={{0,1},{1,2},{2,3},{3,4},{4,5},{5,6},{6,7},{7,8},{8,9},{9,10},{10,1... | collective-permute-start | bytes 552968 | tf_op jit(solution)/shard_map/ppermute | solution.py:44
  121.2 3.4 constant_dynamic-update-slice_fusion
  128.7 6.0 %collective-permute-start.9 = (f32[20,1,32,128]{3,2,1,0:T(8,128)S(1)}, f32[20,1,32,128]{3,2,1,0:T(8,128)S(1)}, u32[]{:S(2)}, u32[]{:S(2)}) collective-permute-start(f32[20,1,32,128]{3,2,1,0:T(8,128)S(1)} %get-tuple-element.123), channel_id=1, source_target_pairs={{16,0},{32,16},{48,32},{64,48},{80,64},{96,80},{112,96},{0,112},{1... | collective-permute-start | bytes 983048 | tf_op jit(solution)/shard_map/ppermute | solution.py:46
  136.4 9.7 %collective-permute-done.8 = f32[20,1,32,128]{3,2,1,0:T(8,128)S(1)} collective-permute-done((f32[20,1,32,128]{3,2,1,0:T(8,128)S(1)}, f32[20,1,32,128]{3,2,1,0:T(8,128)S(1)}, u32[]{:S(2)}, u32[]{:S(2)}) %collective-permute-start.8) | collective-permute-done | bytes 327712 | tf_op jit(solution)/shard_map/ppermute | solution.py:44
  146.1 2.1 collective-permute-done.9
  148.5 2.9 collective-permute-start.10
  151.4 10.4 %collective-permute-start.11 = (f32[20,18,1,128]{3,2,1,0:T(1,128)S(1)}, f32[20,18,1,128]{3,2,1,0:T(1,128)S(1)}, u32[]{:S(2)}, u32[]{:S(2)}) collective-permute-start(f32[20,18,1,128]{3,2,1,0:T(1,128)S(1)} %get-tuple-element.103), channel_id=1, source_target_pairs={{1,0},{2,1},{3,2},{4,3},{5,4},{6,5},{7,6},{8,7},{9,8},{10,9},{11,1... | collective-permute-start | bytes 552968 | tf_op jit(solution)/shard_map/ppermute | solution.py:46
  163.9 23.0 %gather_fusion = f32[4096]{0:T(1024)S(1)} fusion(f32[65536]{0:T(1024)S(1)} %bitcast.599, s32[4096]{0:T(1024)S(1)} %broadcast_clamp_fusion.1), kind=kCustom, calls=%fused_computation | custom fusion | bytes 49152 | tf_op jit(solution)/shard_map/gather | solution.py:162
  187.0 23.0 %gather_fusion.1 = f32[4096]{0:T(1024)S(1)} fusion(f32[65536]{0:T(1024)S(1)} %bitcast.600, s32[4096]{0:T(1024)S(1)} %copy-done.24), kind=kCustom, calls=%fused_computation.1 | custom fusion | bytes 49152 | tf_op jit(solution)/shard_map/gather | solution.py:187
  223.4 39.9 %psum.7 = f32[128]{0:T(128)S(1)} all-reduce(f32[128]{0:T(128)S(1)} %select_reduce_fusion), channel_id=1, replica_groups=mesh['slab'=8,'tile'=16] {'tile'}, use_global_device_ids=true, to_apply=%region_3.4 | all-reduce | flops 128 | bytes 1024 | tf_op jit(solution)/shard_map/psum | solution.py:163
  274.9 3.7 %fusion = f32[128,128]{1,0:T(8,128)S(1)} fusion(bf16[8,128,2048]{2,1,0:T(8,128)(2,1)} %all-gather.4.cloned.1.call-done, bf16[128,2048]{1,0:T(8,128)(2,1)S(1)} %copy-done, f32[128,8]{0,1:T(8,128)S(1)} %fusion.571), kind=kOutput, calls=%fused_computation.4 | convolution fusion | flops 537116672 | bytes 4788224 | tf_op jit(solution)/shard_map/dot_general | solution.py:166
  281.4 24.6 %all-gather.1 = f32[16,1,128]{2,1,0:T(1,128)S(1)} all-gather(f32[1,1,128]{2,1,0:T(1,128)S(1)} %bitcast.640), channel_id=2, replica_groups=mesh['slab'=8,'tile'=16] {'tile'}, dimensions={0}, use_global_device_ids=true | all-gather | bytes 8704 | tf_op jit(solution)/shard_map/all_gather | solution.py:183
  306.3 28.9 %scatter_fusion = f32[65536]{0:T(1024)S(1)} fusion(f32[65536]{0:T(1024)S(1)} %bitcast.601, s32[4096]{0:T(1024)S(1)} %bitcast.639, f32[4096]{0:T(1024)S(1)} %reshape.165), kind=kCustom, calls=%fused_computation.2 | custom fusion | flops 4096 | bytes 65536 | tf_op jit(solution)/shard_map/scatter-add | solution.py:189
  (246 shorter events, 72.4 us)
Async XLA Ops:
  7.2 105.5 %copy-start = (bf16[128,2048]{1,0:T(8,128)(2,1)S(1)}, bf16[128,2048]{1,0:T(8,128)(2,1)}, u32[]{:S(2)}) copy-start(bf16[128,2048]{1,0:T(8,128)(2,1)} %param.19) | copy-start | bytes 1572868
  7.2 267.7 %all-gather.4.cloned.1.call-start = ((), (), s32[]{:S(2)}) async-start(), calls=%async_computation | async-start | bytes 4718592 | tf_op jit(solution)/shard_map/all_gather | solution.py:164
  16.6 37.0 %copy-start.6 = (f32[16,32,128]{2,1,0:T(8,128)}, f32[16,32,128]{2,1,0:T(8,128)S(1)}, u32[]{:S(2)}) copy-start(f32[16,32,128]{2,1,0:T(8,128)S(1)} %get-tuple-element.80) | copy-start | bytes 786436
  16.8 36.0 %copy-start.8 = (f32[16,32,128]{2,1,0:T(8,128)}, f32[16,32,128]{2,1,0:T(8,128)S(1)}, u32[]{:S(2)}) copy-start(f32[16,32,128]{2,1,0:T(8,128)S(1)} %get-tuple-element.78) | copy-start | bytes 786436
  22.1 20.4 %collective-permute-start = (f32[20,1,32,128]{3,2,1,0:T(8,128)S(1)}, f32[20,1,32,128]{3,2,1,0:T(8,128)S(1)}, u32[]{:S(2)}, u32[]{:S(2)}) collective-permute-start(f32[20,1,32,128]{3,2,1,0:T(8,128)S(1)} %get-tuple-element.129), channel_id=1, source_target_pairs={{0,16},{16,32},{32,48},{48,64},{64,80},{80,96},{96,112},{112,0},{1... | collective-permute-start | bytes 983048 | tf_op jit(solution)/shard_map/ppermute | solution.py:44
  23.4 23.2 %collective-permute-start.1 = (f32[20,1,32,128]{3,2,1,0:T(8,128)S(1)}, f32[20,1,32,128]{3,2,1,0:T(8,128)S(1)}, u32[]{:S(2)}, u32[]{:S(2)}) collective-permute-start(f32[20,1,32,128]{3,2,1,0:T(8,128)S(1)} %get-tuple-element.130), channel_id=1, source_target_pairs={{16,0},{32,16},{48,32},{64,48},{80,64},{96,80},{112,96},{0,112},{1... | collective-permute-start | bytes 983048 | tf_op jit(solution)/shard_map/ppermute | solution.py:46
  27.7 24.2 %copy-start.25 = (s32[128,32]{1,0:T(8,128)S(1)}, s32[128,32]{1,0:T(8,128)}, u32[]{:S(2)}) copy-start(s32[128,32]{1,0:T(8,128)} %copy.26) | copy-start | bytes 49156
  49.5 8.3 %collective-permute-start.2 = (f32[20,18,1,128]{3,2,1,0:T(1,128)}, f32[20,18,1,128]{3,2,1,0:T(1,128)S(1)}, u32[]{:S(2)}, u32[]{:S(2)}) collective-permute-start(f32[20,18,1,128]{3,2,1,0:T(1,128)} %get-tuple-element.111), channel_id=1, source_target_pairs={{0,1},{1,2},{2,3},{3,4},{4,5},{5,6},{6,7},{7,8},{8,9},{9,10},{10,1... | collective-permute-start | bytes 552968 | tf_op jit(solution)/shard_map/ppermute | solution.py:44
  51.9 5.9 %collective-permute-start.3 = (f32[20,18,1,128]{3,2,1,0:T(1,128)}, f32[20,18,1,128]{3,2,1,0:T(1,128)}, u32[]{:S(2)}, u32[]{:S(2)}) collective-permute-start(f32[20,18,1,128]{3,2,1,0:T(1,128)} %get-tuple-element.112), channel_id=1, source_target_pairs={{1,0},{2,1},{3,2},{4,3},{5,4},{6,5},{7,6},{8,7},{9,8},{10,9},{11,1... | collective-permute-start | bytes 552968 | tf_op jit(solution)/shard_map/ppermute | solution.py:46
  66.5 49.1 %copy-start.10 = (f32[16,32,128]{2,1,0:T(8,128)}, f32[16,32,128]{2,1,0:T(8,128)S(1)}, u32[]{:S(2)}) copy-start(f32[16,32,128]{2,1,0:T(8,128)S(1)} %get-tuple-element.50) | copy-start | bytes 786436
  66.8 48.8 %copy-start.12 = (f32[16,32,128]{2,1,0:T(8,128)}, f32[16,32,128]{2,1,0:T(8,128)S(1)}, u32[]{:S(2)}) copy-start(f32[16,32,128]{2,1,0:T(8,128)S(1)} %get-tuple-element.48) | copy-start | bytes 786436
  71.9 27.6 %collective-permute-start.4 = (f32[20,1,32,128]{3,2,1,0:T(8,128)S(1)}, f32[20,1,32,128]{3,2,1,0:T(8,128)S(1)}, u32[]{:S(2)}, u32[]{:S(2)}) collective-permute-start(f32[20,1,32,128]{3,2,1,0:T(8,128)S(1)} %get-tuple-element.126), channel_id=1, source_target_pairs={{0,16},{16,32},{32,48},{48,64},{64,80},{80,96},{96,112},{112,0},{1... | collective-permute-start | bytes 983048 | tf_op jit(solution)/shard_map/ppermute | solution.py:44
  73.5 26.0 %collective-permute-start.5 = (f32[20,1,32,128]{3,2,1,0:T(8,128)S(1)}, f32[20,1,32,128]{3,2,1,0:T(8,128)S(1)}, u32[]{:S(2)}, u32[]{:S(2)}) collective-permute-start(f32[20,1,32,128]{3,2,1,0:T(8,128)S(1)} %get-tuple-element.127), channel_id=1, source_target_pairs={{16,0},{32,16},{48,32},{64,48},{80,64},{96,80},{112,96},{0,112},{1... | collective-permute-start | bytes 983048 | tf_op jit(solution)/shard_map/ppermute | solution.py:46
  102.2 16.0 %slice-start.2 = ((s8[5242880]{0:T(1024)(128)(4,1)}), s8[1048576]{0:T(1024)(128)(4,1)S(1)}, s32[]{:S(2)}) async-start(s8[5242880]{0:T(1024)(128)(4,1)} %bitcast.605), calls=%async_computation.3 | async-start | bytes 2097152
  102.2 15.4 %collective-permute-start.6 = (f32[20,18,1,128]{3,2,1,0:T(1,128)}, f32[20,18,1,128]{3,2,1,0:T(1,128)S(1)}, u32[]{:S(2)}, u32[]{:S(2)}) collective-permute-start(f32[20,18,1,128]{3,2,1,0:T(1,128)} %get-tuple-element.107), channel_id=1, source_target_pairs={{0,1},{1,2},{2,3},{3,4},{4,5},{5,6},{6,7},{7,8},{8,9},{9,10},{10,1... | collective-permute-start | bytes 552968 | tf_op jit(solution)/shard_map/ppermute | solution.py:44
  112.7 5.6 %collective-permute-start.7 = (f32[20,18,1,128]{3,2,1,0:T(1,128)}, f32[20,18,1,128]{3,2,1,0:T(1,128)}, u32[]{:S(2)}, u32[]{:S(2)}) collective-permute-start(f32[20,18,1,128]{3,2,1,0:T(1,128)} %get-tuple-element.108), channel_id=1, source_target_pairs={{1,0},{2,1},{3,2},{4,3},{5,4},{6,5},{7,6},{8,7},{9,8},{10,9},{11,1... | collective-permute-start | bytes 552968 | tf_op jit(solution)/shard_map/ppermute | solution.py:46
  128.6 34.7 %copy-start.2 = (f32[20,16,32,128]{3,2,1,0:T(8,128)}, f32[20,16,32,128]{3,2,1,0:T(8,128)S(1)}, u32[]{:S(2)}) copy-start(f32[20,16,32,128]{3,2,1,0:T(8,128)S(1)} %bitcast_dynamic-update-slice_fusion) | copy-start | bytes 15728644
  128.6 17.5 %collective-permute-start.8 = (f32[20,1,32,128]{3,2,1,0:T(8,128)S(1)}, f32[20,1,32,128]{3,2,1,0:T(8,128)S(1)}, u32[]{:S(2)}, u32[]{:S(2)}) collective-permute-start(f32[20,1,32,128]{3,2,1,0:T(8,128)S(1)} %get-tuple-element.124), channel_id=1, source_target_pairs={{0,16},{16,32},{32,48},{48,64},{64,80},{80,96},{96,112},{112,0},{1... | collective-permute-start | bytes 983048 | tf_op jit(solution)/shard_map/ppermute | solution.py:44
  128.7 19.5 %collective-permute-start.9 = (f32[20,1,32,128]{3,2,1,0:T(8,128)S(1)}, f32[20,1,32,128]{3,2,1,0:T(8,128)S(1)}, u32[]{:S(2)}, u32[]{:S(2)}) collective-permute-start(f32[20,1,32,128]{3,2,1,0:T(8,128)S(1)} %get-tuple-element.123), channel_id=1, source_target_pairs={{16,0},{32,16},{48,32},{64,48},{80,64},{96,80},{112,96},{0,112},{1... | collective-permute-start | bytes 983048 | tf_op jit(solution)/shard_map/ppermute | solution.py:46
  148.5 14.7 %collective-permute-start.10 = (f32[20,18,1,128]{3,2,1,0:T(1,128)S(1)}, f32[20,18,1,128]{3,2,1,0:T(1,128)S(1)}, u32[]{:S(2)}, u32[]{:S(2)}) collective-permute-start(f32[20,18,1,128]{3,2,1,0:T(1,128)S(1)} %get-tuple-element.104), channel_id=1, source_target_pairs={{0,1},{1,2},{2,3},{3,4},{4,5},{5,6},{6,7},{7,8},{8,9},{9,10},{10,1... | collective-permute-start | bytes 552968 | tf_op jit(solution)/shard_map/ppermute | solution.py:44
  151.4 11.9 %collective-permute-start.11 = (f32[20,18,1,128]{3,2,1,0:T(1,128)S(1)}, f32[20,18,1,128]{3,2,1,0:T(1,128)S(1)}, u32[]{:S(2)}, u32[]{:S(2)}) collective-permute-start(f32[20,18,1,128]{3,2,1,0:T(1,128)S(1)} %get-tuple-element.103), channel_id=1, source_target_pairs={{1,0},{2,1},{3,2},{4,3},{5,4},{6,5},{7,6},{8,7},{9,8},{10,9},{11,1... | collective-permute-start | bytes 552968 | tf_op jit(solution)/shard_map/ppermute | solution.py:46
  163.9 23.1 %copy-start.24 = (s32[4096]{0:T(1024)S(1)}, s32[4096]{0:T(1024)}, u32[]{:S(2)}) copy-start(s32[4096]{0:T(1024)} %broadcast_clamp_fusion) | copy-start | bytes 49156
  265.2 40.9 %copy-start.32 = (pred[128,32]{1,0:T(8,128)(4,1)S(1)}, pred[128,32]{1,0:T(8,128)(4,1)}, u32[]{:S(2)}) copy-start(pred[128,32]{1,0:T(8,128)(4,1)} %get-tuple-element.16) | copy-start | bytes 12292
  267.0 39.2 %copy-start.29 = (s32[4096,1]{0,1:T(1,128)S(1)}, s32[4096,1]{0,1:T(1,128)}, u32[]{:S(2)}) copy-start(s32[4096,1]{0,1:T(1,128)} %compare_select_fusion.2) | copy-start | bytes 49156
  (28 other events, 99.2 us)
Sparse Core Ops, SparseCore 0:
  24.7 119.5 all-gather.3
